TPU v7x, 512 devices: a whole 4x8x8 slice. The times are simulated.
512 devices in a mesh: depth: 16 (over x, z_hi), plane: 32 (over z_lo, y, core).
Axes of the slice: x: 4, y: 8, z: 8 (z_hi: 4, z_lo: 2; z = z_hi * 2 + z_lo), core: 2. Of those that a mesh axis runs over, the one named last changes fastest.
Arguments:
- volume: bfloat16 [64, 128, 128], P('depth', 'plane'), may hold values from -6 to 6
- cotangent: float32 [64, 128, 128], P('depth', 'plane'), may hold values from -6 to 6
- kernel_in: bfloat16 [27, 32], replicated, may hold values from -1.25 to 1.25
- kernel_mid: bfloat16 [27, 32, 32], replicated, may hold values from -0.21875 to 0.21875
- kernel_out: bfloat16 [27, 32], replicated, may hold values from -0.21875 to 0.21875
- measured: float32 [64, 32, 1024], P('depth'), may hold values from -24 to 24
- angle_ids: int32 [8], replicated, may hold values from 0 to 31, as said below
- ray_bins: int32 [8, 128, 128], P(None, 'plane'), may hold values from 0 to 1023, as said below
Outputs:
- grad_volume: float32 [64, 128, 128], P('depth', 'plane')
- grad_kernel_in: float32 [27, 32], replicated
- grad_kernel_mid: float32 [27, 32, 32], replicated
- grad_kernel_out: float32 [27, 32], replicated
Inputs may be any that keep to these rules, and one draw needn't show every extreme that they name: `angle_ids`: each entry names a measured view; the entries are distinct. `ray_bins`: for each view a, the bins follow parallel-beam geometry: a cell's bin is the detector position of its centre projected along the direction of view angle_ids[a], clipped at the detector's ends.
All inputs are finite; a program needn't handle non-finite values.
Results may differ from a plain program's by a relative error of at most 0.0051.
Values may be sent and summed in bfloat16 or wider, within the bound.
No kernel may reach another device: no remote copies, remote signals or barrier semaphores. Data moves between devices by JAX's collectives and lax.ppermute only.
A program may use at most 64 MiB of HBM per device.

v0:
```python
import jax
import jax.numpy as jnp
from jax import lax
from jax.sharding import PartitionSpec as P

BINS = 1024
ANG = 8
delta_scale = 6.0


def extended(cells, sides, width):
    for axis, dim in sides:
        count = lax.axis_size(axis)
        ends = count - 1
        head = lax.slice_in_dim(cells, 0, width, axis=dim)
        tail = lax.slice_in_dim(cells, cells.shape[dim] - width, cells.shape[dim], axis=dim)
        cells = jnp.concatenate(
            [
                lax.ppermute(tail, axis, [(i, (i + 1) % count) for i in range(ends)]),
                cells,
                lax.ppermute(head, axis, [((i + 1) % count, i) for i in range(ends)]),
            ],
            axis=dim,
        )
    return cells


def shifts():
    return [
        (step_z, step_y, step_x)
        for step_z in (-1, 0, 1)
        for step_y in (-1, 0, 1)
        for step_x in (-1, 0, 1)
    ]


def pad_row(field):
    return jnp.pad(field, ((0, 0), (0, 0), (0, 0), (1, 1)))


def extend(field):
    padded = extended(field, (("depth", 1), ("plane", 2)), 1)
    return pad_row(padded)


def window_at(padded, start_z, start_y, start_x, extent):
    return lax.slice(
        padded,
        (0, start_z, start_y, start_x),
        (padded.shape[0], start_z + extent[0], start_y + extent[1], start_x + extent[2]),
    )


def forward_conv(padded, kernel, extent, base):
    summed = jnp.zeros((kernel.shape[1],) + tuple(extent), jnp.float32)
    for position, (step_z, step_y, step_x) in enumerate(shifts()):
        window = window_at(padded, base[0] + step_z, base[1] + step_y, base[2] + step_x, extent)
        summed = summed + jnp.einsum(
            "oc,czhw->ozhw", kernel[position], window, preferred_element_type=jnp.float32
        )
    return summed


def adjoint_conv(padded, kernel, extent, base):
    summed = jnp.zeros((kernel.shape[2],) + tuple(extent), jnp.float32)
    for position, (step_z, step_y, step_x) in enumerate(shifts()):
        window = window_at(padded, base[0] - step_z, base[1] - step_y, base[2] - step_x, extent)
        summed = summed + jnp.einsum(
            "oc,ozhw->czhw", kernel[position], window, preferred_element_type=jnp.float32
        )
    return summed


def kernel_grad(grad_out, padded_in, extent, base):
    pieces = []
    for position, (step_z, step_y, step_x) in enumerate(shifts()):
        window = window_at(padded_in, base[0] + step_z, base[1] + step_y, base[2] + step_x, extent)
        pieces.append(
            jnp.einsum("ozhw,czhw->oc", grad_out, window, preferred_element_type=jnp.float32)
        )
    return jnp.stack(pieces)


def silu_slope(value):
    sigma = jax.nn.sigmoid(value)
    return sigma * (1.0 + value * (1.0 - sigma))


def project_pair(first, second, ray_bins):
    slices = first.shape[0]
    flattened = jnp.concatenate((first.reshape(slices, -1), second.reshape(slices, -1)), axis=0).T

    def one_view(bins_view):
        return jax.ops.segment_sum(flattened, bins_view.reshape(-1), num_segments=BINS)

    per_view = lax.map(one_view, ray_bins)
    stacked = jnp.transpose(per_view, (2, 0, 1))
    return (stacked[:slices], stacked[slices:])


def back_project(rays, ray_bins):

    def accumulate(summed, view_pair):
        rays_view, bins_view = view_pair
        return (summed + jnp.take(rays_view, bins_view.reshape(-1), axis=1), None)

    initial = jnp.zeros((rays.shape[0], ray_bins.shape[1] * ray_bins.shape[2]), rays.dtype)
    summed = lax.scan(accumulate, initial, (jnp.transpose(rays, (1, 0, 2)), ray_bins))[0]
    return summed.reshape(rays.shape[0], ray_bins.shape[1], ray_bins.shape[2])


def curvature(residual):
    ratio = residual / delta_scale
    inner = 1.0 + ratio * ratio
    return 1.0 / (inner * jnp.sqrt(inner))


def per_device(volume, cotangent, kernel_in, kernel_mid, kernel_out, measured, angle_ids, ray_bins):
    extent = volume.shape
    depth_rows, plane_rows, cells = extent
    first_in = kernel_in[:, :, None]
    last_out = kernel_out[:, None, :]
    source_pad = extend(volume[None])
    first_raw = forward_conv(source_pad, first_in, extent, (1, 1, 1))
    act_first = jax.nn.silu(first_raw).astype(jnp.bfloat16)
    slope_first = silu_slope(first_raw)
    first_pad = extend(act_first)
    second_raw = forward_conv(first_pad, kernel_mid, extent, (1, 1, 1))
    act_second = jax.nn.silu(second_raw).astype(jnp.bfloat16)
    slope_second = silu_slope(second_raw)
    second_pad = extend(act_second)
    residue = forward_conv(second_pad, last_out, extent, (1, 1, 1))[0]
    source_margin, first_margin, second_margin = (1, 1, 1)
    mid_margin, low_margin = (0, 0)
    denoised = volume.astype(jnp.float32) - residue
    chosen = jnp.take(measured, angle_ids, axis=1)
    local_rays, local_cot = project_pair(denoised, cotangent, ray_bins)
    forward_rays, cot_rays = lax.psum((local_rays, local_cot), "plane")
    weighted = curvature(forward_rays - chosen) * cot_rays
    grad_denoised = cotangent - 0.25 / ANG * back_project(weighted, ray_bins)
    cell_count = depth_rows * lax.axis_size("depth") * plane_rows * lax.axis_size("plane") * cells
    grad_scale = float(cell_count) ** (-0.5)
    grad_last = (-grad_denoised).astype(jnp.bfloat16)
    last_pad = extend(grad_last[None])
    mid_extent = (depth_rows + 2 * mid_margin, plane_rows + 2 * mid_margin, cells)
    low_extent = (depth_rows + 2 * low_margin, plane_rows + 2 * low_margin, cells)
    term_out = kernel_grad(grad_last[None], second_pad, extent, (second_margin, second_margin, 1))[
        :, 0, :
    ]
    grad_second = adjoint_conv(last_pad, last_out, mid_extent, (1, 1, 1))
    grad_mid = (grad_second * slope_second).astype(jnp.bfloat16)
    term_mid = kernel_grad(grad_mid, first_pad, extent, (first_margin, first_margin, 1))
    mid_pad = extend(grad_mid)
    grad_first = adjoint_conv(mid_pad, kernel_mid, low_extent, (1, 1, 1))
    grad_low = (grad_first * slope_first).astype(jnp.bfloat16)
    term_in = kernel_grad(grad_low, source_pad, extent, (source_margin, source_margin, 1))[:, :, 0]
    term_in, term_mid, term_out = lax.psum((term_in, term_mid, term_out), ("depth", "plane"))
    low_pad = extend(grad_low)
    grad_volume = grad_denoised + adjoint_conv(low_pad, first_in, extent, (1, 1, 1))[0]
    return (grad_volume, term_in * grad_scale, term_mid * grad_scale, term_out * grad_scale)


def solution(mesh):
    placed = (
        P("depth", "plane", None),
        P("depth", "plane", None),
        P(),
        P(),
        P(),
        P("depth", None, None),
        P(),
        P(None, "plane", None),
    )
    return jax.shard_map(
        per_device,
        mesh=mesh,
        in_specs=placed,
        out_specs=(P("depth", "plane", None), P(), P(), P()),
        check_vma=False,
    )
```

profile of v0, /device:TPU:64, one launch (start us, length us, event | category | flops | bytes accessed | tf_op | source)
XLA Modules:
  0.0 829.1 jit_solution(6284097332181020481)
XLA Ops:
  8.0 6.1 collective-permute-start
  25.7 5.8 collective-permute-start.3
  36.5 7.0 collective-permute-start.4
  45.6 5.9 collective-permute-done.5
  53.5 5.9 collective-permute-start.7
  70.3 5.9 collective-permute-start.8
  77.9 5.1 collective-permute-done.9
  84.9 5.8 collective-permute-start.11
  99.5 32.3 %while.21 = (s32[]{:T(128)}, f32[8,1024,8]{1,0,2:T(8,128)S(1)}, s32[8,4,128]{2,1,0:T(4,128)}, f32[512,8]{1,0:T(8,128)}, s32[]{:T(128)}, /*index=5*/f32[]{:T(128)}, s32[]{:T(128)}) while((s32[]{:T(128)}, f32[8,1024,8]{1,0,2:T(8,128)S(1)}, s32[8,4,128]{2,1,0:T(4,128)}, f32[512,8]{1,0:T(8,128)}, s32[]{:T(128)}, /*index=5*/f32[]{:T(128)}, ...), condition=%wide.region_2.3_spmd, body=%wide.region_0.2_spmd.sunk | while | flops 4098 | bytes 168533 | solution.py:96
  100.2 2.8 scatter_custom_fusion.5
  111.6 4.6 scatter_custom_fusion.5
  117.3 2.8 scatter_custom_fusion.5
  134.1 226.0 %all-reduce.13.cloned.1.call-done = (f32[4,8,1024]{2,1,0:T(8,128)}, f32[4,8,1024]{2,1,0:T(8,128)}) async-done(((f32[4,8,1024]{2,1,0:T(8,128)}, f32[4,8,1024]{2,1,0:T(8,128)}), (f32[4,8,1024]{2,1,0:T(8,128)}, f32[4,8,1024]{2,1,0:T(8,128)})) %all-reduce.13.cloned.1.call-update) | async-done | bytes 262160 | tf_op jit(solution)/shard_map/psum | solution.py:138
  361.2 17.5 %while.22 = (s32[]{:T(128)}, f32[4,512]{0,1:T(8,128)S(1)}, s32[8,4,128]{2,1,0:T(4,128)}, f32[8,4,1024]{2,0,1:T(8,128)S(1)}, s32[]{:T(128)}, /*index=5*/s32[]{:T(128)}) while((s32[]{:T(128)}, f32[4,512]{0,1:T(8,128)S(1)}, s32[8,4,128]{2,1,0:T(4,128)}, f32[8,4,1024]{2,0,1:T(8,128)S(1)}, s32[]{:T(128)}, /*index=5*/s32[]{:T(128)}) %tuple.247), condition=%wide.region_6.7_spmd.clone, body=%wide.region_5.6_spmd.clone.sunk | while | flops 11779 | bytes 123991 | solution.py:108
  379.0 4.8 collective-permute-start.12
  392.2 5.8 collective-permute-start.15
  406.9 6.2 collective-permute-start.16
  415.9 4.3 collective-permute-done.17
  420.2 4.6 collective-permute-start.19
  426.9 260.4 %all-reduce.11.cloned.1.call-done = f32[27,32,32]{2,1,0:T(8,128)} async-done(((f32[27,32,32]{2,1,0:T(8,128)}), f32[27,32,32]{2,1,0:T(8,128)}) %all-reduce.11.cloned.1.call-update) | async-done | bytes 110608 | tf_op jit(solution)/shard_map/psum | solution.py:157
  700.6 95.3 %all-reduce.6 = (f32[27,32]{1,0:T(8,128)S(1)}, f32[27,32]{1,0:T(8,128)S(1)}) all-reduce(f32[27,32]{1,0:T(8,128)S(1)} %bitcast.2037, f32[27,32]{1,0:T(8,128)S(1)} %bitcast.2036), channel_id=1, replica_groups=mesh['depth'=16,'plane'=32] {'depth','plane'}, use_global_device_ids=true, to_apply=%region_7.8 | all-reduce | flops 1728 | bytes 13824 | tf_op jit(solution)/shard_map/psum | solution.py:157
  796.5 4.6 collective-permute-start.20
  803.0 4.8 collective-permute-done.21
  812.4 4.8 collective-permute-done.22
  (574 shorter events, 133.5 us)
Async XLA Ops:
  7.2 352.9 %all-reduce.13.cloned.1.call-start = ((), (), s32[]{:S(2)}) async-start(), calls=%async_computation.1 | async-start | bytes 524288 | tf_op jit(solution)/shard_map/psum | solution.py:138
  8.0 15.0 %collective-permute-start = (bf16[1,1,4,128]{3,2,1,0:T(4,128)(2,1)S(1)}, bf16[1,1,4,128]{3,2,1,0:T(4,128)(2,1)S(1)}, u32[]{:S(2)}, u32[]{:S(2)}) collective-permute-start(bf16[1,1,4,128]{3,2,1,0:T(4,128)(2,1)S(1)} %get-tuple-element.323), channel_id=1, source_target_pairs={{0,32},{32,64},{64,96},{96,128},{128,160},{160,192},{192,224},{224... | collective-permute-start | bytes 3080 | tf_op jit(solution)/shard_map/ppermute | solution.py:19
  14.1 9.0 %collective-permute-start.1 = (bf16[1,1,4,128]{3,2,1,0:T(4,128)(2,1)S(1)}, bf16[1,1,4,128]{3,2,1,0:T(4,128)(2,1)S(1)}, u32[]{:S(2)}, u32[]{:S(2)}) collective-permute-start(bf16[1,1,4,128]{3,2,1,0:T(4,128)(2,1)S(1)} %get-tuple-element.324), channel_id=1, source_target_pairs={{32,0},{64,32},{96,64},{128,96},{160,128},{192,160},{224,192},{256... | collective-permute-start | bytes 3080 | tf_op jit(solution)/shard_map/ppermute | solution.py:21
  23.7 9.1 %collective-permute-start.2 = (bf16[1,6,1,128]{3,2,1,0:T(2,128)(2,1)S(1)}, bf16[1,6,1,128]{3,2,1,0:T(2,128)(2,1)S(1)}, u32[]{:S(2)}, u32[]{:S(2)}) collective-permute-start(bf16[1,6,1,128]{3,2,1,0:T(2,128)(2,1)S(1)} %get-tuple-element.311), channel_id=1, source_target_pairs={{0,1},{1,2},{2,3},{3,4},{4,5},{5,6},{6,7},{7,8},{8,9},{9,10},{10,1... | collective-permute-start | bytes 4616 | tf_op jit(solution)/shard_map/ppermute | solution.py:19
  25.7 7.1 collective-permute-start.3
  36.5 9.2 %collective-permute-start.4 = (bf16[32,1,4,128]{3,0,2,1:T(8,128)(2,1)S(1)}, bf16[32,1,4,128]{3,0,2,1:T(8,128)(2,1)S(1)}, u32[]{:S(2)}, u32[]{:S(2)}) collective-permute-start(bf16[32,1,4,128]{3,0,2,1:T(8,128)(2,1)S(1)} %get-tuple-element.175), channel_id=1, source_target_pairs={{0,32},{32,64},{64,96},{96,128},{128,160},{160,192},{192,224},{224... | collective-permute-start | bytes 98312 | tf_op jit(solution)/shard_map/ppermute | solution.py:19
  43.5 8.0 collective-permute-start.5
  51.5 7.9 collective-permute-start.6
  53.5 7.6 collective-permute-start.7
  70.3 7.5 collective-permute-start.8
  76.3 6.7 collective-permute-start.9
  83.0 8.7 %collective-permute-start.10 = (bf16[32,6,1,128]{3,0,2,1:T(8,128)(2,1)S(1)}, bf16[32,6,1,128]{3,0,2,1:T(8,128)(2,1)S(1)}, u32[]{:S(2)}, u32[]{:S(2)}) collective-permute-start(bf16[32,6,1,128]{3,0,2,1:T(8,128)(2,1)S(1)} %get-tuple-element.159), channel_id=1, source_target_pairs={{0,1},{1,2},{2,3},{3,4},{4,5},{5,6},{6,7},{7,8},{8,9},{9,10},{10,1... | collective-permute-start | bytes 147464 | tf_op jit(solution)/shard_map/ppermute | solution.py:19
  84.9 7.5 collective-permute-start.11
  132.6 554.8 %all-reduce.11.cloned.1.call-start = ((), (), s32[]{:S(2)}) async-start(), calls=%async_computation | async-start | bytes 884736 | tf_op jit(solution)/shard_map/psum | solution.py:157
  379.0 10.9 %collective-permute-start.12 = (bf16[1,1,4,128]{3,2,1,0:T(4,128)(2,1)S(1)}, bf16[1,1,4,128]{3,2,1,0:T(4,128)(2,1)S(1)}, u32[]{:S(2)}, u32[]{:S(2)}) collective-permute-start(bf16[1,1,4,128]{3,2,1,0:T(4,128)(2,1)S(1)} %get-tuple-element.321), channel_id=1, source_target_pairs={{0,32},{32,64},{64,96},{96,128},{128,160},{160,192},{192,224},{224... | collective-permute-start | bytes 3080 | tf_op jit(solution)/shard_map/ppermute | solution.py:19
  383.8 6.5 collective-permute-start.13
  390.3 7.7 collective-permute-start.14
  392.2 7.1 collective-permute-start.15
  406.9 9.0 %collective-permute-start.16 = (bf16[32,1,4,128]{3,0,2,1:T(8,128)(2,1)S(1)}, bf16[32,1,4,128]{3,0,2,1:T(8,128)(2,1)S(1)}, u32[]{:S(2)}, u32[]{:S(2)}) collective-permute-start(bf16[32,1,4,128]{3,0,2,1:T(8,128)(2,1)S(1)} %get-tuple-element.169), channel_id=1, source_target_pairs={{0,32},{32,64},{64,96},{96,128},{128,160},{160,192},{192,224},{224... | collective-permute-start | bytes 98312 | tf_op jit(solution)/shard_map/ppermute | solution.py:19
  413.1 7.1 collective-permute-start.17
  420.2 269.0 %collective-permute-start.19 = (bf16[32,6,1,128]{3,0,2,1:T(8,128)(2,1)S(1)}, bf16[32,6,1,128]{3,0,2,1:T(8,128)(2,1)S(1)}, u32[]{:S(2)}, u32[]{:S(2)}) collective-permute-start(bf16[32,6,1,128]{3,0,2,1:T(8,128)(2,1)S(1)} %get-tuple-element.156), channel_id=1, source_target_pairs={{1,0},{2,1},{3,2},{4,3},{5,4},{6,5},{7,6},{8,7},{9,8},{10,9},{11,1... | collective-permute-start | bytes 147464 | tf_op jit(solution)/shard_map/ppermute | solution.py:21
  424.8 264.4 %collective-permute-start.18 = (bf16[32,6,1,128]{3,0,2,1:T(8,128)(2,1)S(1)}, bf16[32,6,1,128]{3,0,2,1:T(8,128)(2,1)S(1)}, u32[]{:S(2)}, u32[]{:S(2)}) collective-permute-start(bf16[32,6,1,128]{3,0,2,1:T(8,128)(2,1)S(1)} %get-tuple-element.155), channel_id=1, source_target_pairs={{0,1},{1,2},{2,3},{3,4},{4,5},{5,6},{6,7},{7,8},{8,9},{9,10},{10,1... | collective-permute-start | bytes 147464 | tf_op jit(solution)/shard_map/ppermute | solution.py:19
  801.1 6.7 collective-permute-start.21
  809.8 7.5 collective-permute-start.22
  (99 other events, 719.6 us)
Sparse Core Ops, SparseCore 0:
  132.7 227.3 all-reduce.12
  416.0 271.3 all-reduce.10
where the time goes:
time: 831 us; the launch traced here: 829 us
  waiting for transfers between devices  516 us (62%)
  blocking collectives  95.3 us (11%)
  starting transfers between devices  84.2 us (10%)
  other arithmetic  52.3 us (6%)
  matrix products  32.7 us (4%)
  local copies, waits for them, and re-layouts  32.5 us (4%)
  between operations  15.8 us (2%)
    psum x1, waiting for transfers between devices, per_device(): lax.psum((term_in, term_mid, term_out), ('depth', 'plane'))  260 us
    psum x1, waiting for transfers between devices, per_device(): forward_rays, cot_rays = lax.psum((local_rays, local_cot), 'plane')  226 us
    psum x1, blocking collectives, per_device(): lax.psum((term_in, term_mid, term_out), ('depth', 'plane'))  95.3 us
    ppermute x12, starting transfers between devices, extended(): lax.ppermute(tail, axis, [(i, (i + 1) % count) for i in range(ends)])  46.5 us
    ppermute x12, starting transfers between devices, extended(): lax.ppermute(head, axis, [((i + 1) % count, i) for i in range(ends)])  37.6 us
    ppermute x12, waiting for transfers between devices, extended(): lax.ppermute(head, axis, [((i + 1) % count, i) for i in range(ends)])  24.2 us
    scatter-add x8, other arithmetic, one_view(): jax.ops.segment_sum(flattened, bins_view.reshape(-1), num_segments=BINS)  24 us
  transfers between devices with their start and end apart: 26, of which 12 were waited for; matrix products, arithmetic and copies ran while one was open for 2% of the time, Pallas kernels for 0%

commit v1 on v0

--- a/solution.py
+++ b/solution.py
@@ -1,3 +1,4 @@
+import functools
 import jax
 import jax.numpy as jnp
 from jax import lax
@@ -6,6 +7,15 @@
 BINS = 1024
 ANG = 8
 delta_scale = 6.0
+
+
+def track_packet(sheet, along_axis, named_axis):
+    for b in (along_axis, named_axis):
+        sheet = lax.psum(sheet, axis_name=b)
+    return sheet
+
+
+perform_frames = functools.partial(track_packet, along_axis="depth", named_axis="plane")
 
 
 def extended(cells, sides, width):
@@ -154,7 +164,7 @@
     grad_first = adjoint_conv(mid_pad, kernel_mid, low_extent, (1, 1, 1))
     grad_low = (grad_first * slope_first).astype(jnp.bfloat16)
     term_in = kernel_grad(grad_low, source_pad, extent, (source_margin, source_margin, 1))[:, :, 0]
-    term_in, term_mid, term_out = lax.psum((term_in, term_mid, term_out), ("depth", "plane"))
+    term_in, term_mid, term_out = perform_frames((term_in, term_mid, term_out))
     low_pad = extend(grad_low)
     grad_volume = grad_denoised + adjoint_conv(low_pad, first_in, extent, (1, 1, 1))[0]
     return (grad_volume, term_in * grad_scale, term_mid * grad_scale, term_out * grad_scale)

time: 831 us -> 865 us (1.041)
  the two profiles are of different devices: /device:TPU:64 before, /device:TPU:1 now
where the time goes in v1:
time: 865 us; the launch traced here: 863 us
  waiting for transfers between devices  464 us (54%)
  blocking collectives  185 us (21%)
  starting transfers between devices  74.8 us (9%)
  other arithmetic  55.7 us (6%)
  matrix products  34.3 us (4%)
  local copies, waits for them, and re-layouts  32.4 us (4%)
  between operations  15.5 us (2%)
    psum x1, waiting for transfers between devices, per_device(): forward_rays, cot_rays = lax.psum((local_rays, local_cot), 'plane')  227 us
    psum x2, waiting for transfers between devices, track_packet(): sheet = lax.psum(sheet, axis_name=b)  209 us
    psum x2, blocking collectives, track_packet(): sheet = lax.psum(sheet, axis_name=b)  185 us
    ppermute x12, starting transfers between devices, extended(): lax.ppermute(tail, axis, [(i, (i + 1) % count) for i in range(ends)])  49 us
    scatter-add x8, other arithmetic, one_view(): jax.ops.segment_sum(flattened, bins_view.reshape(-1), num_segments=BINS)  27.5 us
    ppermute x12, waiting for transfers between devices, extended(): lax.ppermute(head, axis, [((i + 1) % count, i) for i in range(ends)])  26.6 us
    ppermute x12, starting transfers between devices, extended(): lax.ppermute(head, axis, [((i + 1) % count, i) for i in range(ends)])  25.7 us
  transfers between devices with their start and end apart: 27, of which 12 were waited for; matrix products, arithmetic and copies ran while one was open for 4% of the time, Pallas kernels for 0%

profile of v1, /device:TPU:1, one launch (start us, length us, event | category | flops | bytes accessed | tf_op | source)
XLA Modules:
  0.0 863.1 jit_solution(5156873765815244062)
XLA Ops:
  8.0 6.6 collective-permute-start
  24.3 4.0 collective-permute-start.2
  37.0 7.6 collective-permute-start.4
  46.7 4.9 collective-permute-done.5
  57.0 3.4 collective-permute-done.7
  69.6 5.8 collective-permute-start.8
  76.8 4.1 collective-permute-done.9
  81.0 3.3 collective-permute-start.10
  96.8 35.7 %while.21 = (s32[]{:T(128)}, f32[8,1024,8]{1,0,2:T(8,128)S(1)}, s32[8,4,128]{2,1,0:T(4,128)}, f32[512,8]{1,0:T(8,128)}, s32[]{:T(128)}, /*index=5*/f32[]{:T(128)}, s32[]{:T(128)}) while((s32[]{:T(128)}, f32[8,1024,8]{1,0,2:T(8,128)S(1)}, s32[8,4,128]{2,1,0:T(4,128)}, f32[512,8]{1,0:T(8,128)}, s32[]{:T(128)}, /*index=5*/f32[]{:T(128)}, ...), condition=%wide.region_2.3_spmd, body=%wide.region_0.2_spmd.sunk | while | flops 4098 | bytes 168533 | solution.py:106
  97.5 3.5 scatter_custom_fusion.5
  110.5 4.6 scatter_custom_fusion.5
  120.2 3.3 scatter_custom_fusion.5
  124.5 3.5 scatter_custom_fusion.5
  134.8 227.3 %all-reduce.17.cloned.1.call-done = (f32[4,8,1024]{2,1,0:T(8,128)}, f32[4,8,1024]{2,1,0:T(8,128)}) async-done(((f32[4,8,1024]{2,1,0:T(8,128)}, f32[4,8,1024]{2,1,0:T(8,128)}), (f32[4,8,1024]{2,1,0:T(8,128)}, f32[4,8,1024]{2,1,0:T(8,128)})) %all-reduce.17.cloned.1.call-update) | async-done | bytes 262160 | tf_op jit(solution)/shard_map/psum | solution.py:148
  363.2 17.5 %while.22 = (s32[]{:T(128)}, f32[4,512]{0,1:T(8,128)S(1)}, s32[8,4,128]{2,1,0:T(4,128)}, f32[8,4,1024]{2,0,1:T(8,128)S(1)}, s32[]{:T(128)}, /*index=5*/s32[]{:T(128)}) while((s32[]{:T(128)}, f32[4,512]{0,1:T(8,128)S(1)}, s32[8,4,128]{2,1,0:T(4,128)}, f32[8,4,1024]{2,0,1:T(8,128)S(1)}, s32[]{:T(128)}, /*index=5*/s32[]{:T(128)}) %tuple.249), condition=%wide.region_6.7_spmd.clone, body=%wide.region_5.6_spmd.clone.sunk | while | flops 11779 | bytes 123991 | solution.py:118
  381.0 4.5 collective-permute-start.12
  407.7 5.4 collective-permute-start.16
  416.0 3.9 collective-permute-done.17
  422.2 3.4 collective-permute-start.18
  438.1 68.5 %all-reduce.8 = (f32[27,32]{1,0:T(8,128)S(1)}, f32[27,32]{1,0:T(8,128)S(1)}) all-reduce(f32[27,32]{1,0:T(8,128)S(1)} %bitcast.2037, f32[27,32]{1,0:T(8,128)S(1)} %bitcast.2036), channel_id=1, replica_groups=mesh['depth'=16,'plane'=32] {'depth'}, use_global_device_ids=true, to_apply=%region_7.8 | all-reduce | flops 1728 | bytes 13824 | tf_op jit(solution)/shard_map/psum | solution.py:14
  506.6 116.8 %all-reduce.6 = (f32[27,32]{1,0:T(8,128)S(1)}, f32[27,32]{1,0:T(8,128)S(1)}) all-reduce(f32[27,32]{1,0:T(8,128)S(1)} %get-tuple-element.97, f32[27,32]{1,0:T(8,128)S(1)} %get-tuple-element.98), channel_id=1, replica_groups=mesh['depth'=16,'plane'=32] {'plane'}, use_global_device_ids=true, to_apply=%region_8.9 | all-reduce | flops 1728 | bytes 13824 | tf_op jit(solution)/shard_map/psum | solution.py:14
  627.2 3.6 collective-permute-done.21
  630.8 7.3 collective-permute-start.23
  646.2 208.6 %all-reduce.15.cloned.1.call-done = f32[27,32,32]{2,1,0:T(8,128)} async-done(((f32[27,32,32]{2,1,0:T(8,128)}), f32[27,32,32]{2,1,0:T(8,128)}) %all-reduce.15.cloned.1.call-update) | async-done | bytes 110608 | tf_op jit(solution)/shard_map/psum | solution.py:14
  (584 shorter events, 142.9 us)
Async XLA Ops:
  7.2 354.9 %all-reduce.17.cloned.1.call-start = ((), (), s32[]{:S(2)}) async-start(), calls=%async_computation.2 | async-start | bytes 524288 | tf_op jit(solution)/shard_map/psum | solution.py:148
  8.0 15.6 %collective-permute-start = (bf16[1,1,4,128]{3,2,1,0:T(4,128)(2,1)S(1)}, bf16[1,1,4,128]{3,2,1,0:T(4,128)(2,1)S(1)}, u32[]{:S(2)}, u32[]{:S(2)}) collective-permute-start(bf16[1,1,4,128]{3,2,1,0:T(4,128)(2,1)S(1)} %get-tuple-element.325), channel_id=1, source_target_pairs={{0,32},{32,64},{64,96},{96,128},{128,160},{160,192},{192,224},{224... | collective-permute-start | bytes 3080 | tf_op jit(solution)/shard_map/ppermute | solution.py:29
  14.6 9.0 %collective-permute-start.1 = (bf16[1,1,4,128]{3,2,1,0:T(4,128)(2,1)S(1)}, bf16[1,1,4,128]{3,2,1,0:T(4,128)(2,1)S(1)}, u32[]{:S(2)}, u32[]{:S(2)}) collective-permute-start(bf16[1,1,4,128]{3,2,1,0:T(4,128)(2,1)S(1)} %get-tuple-element.326), channel_id=1, source_target_pairs={{32,0},{64,32},{96,64},{128,96},{160,128},{192,160},{224,192},{256... | collective-permute-start | bytes 3080 | tf_op jit(solution)/shard_map/ppermute | solution.py:31
  24.3 7.3 collective-permute-start.2
  28.4 4.9 collective-permute-start.3
  37.0 9.8 %collective-permute-start.4 = (bf16[32,1,4,128]{3,0,2,1:T(8,128)(2,1)S(1)}, bf16[32,1,4,128]{3,0,2,1:T(8,128)(2,1)S(1)}, u32[]{:S(2)}, u32[]{:S(2)}) collective-permute-start(bf16[32,1,4,128]{3,0,2,1:T(8,128)(2,1)S(1)} %get-tuple-element.177), channel_id=1, source_target_pairs={{0,32},{32,64},{64,96},{96,128},{128,160},{160,192},{192,224},{224... | collective-permute-start | bytes 98312 | tf_op jit(solution)/shard_map/ppermute | solution.py:29
  44.6 7.1 collective-permute-start.5
  51.7 5.3 collective-permute-start.6
  54.9 5.5 collective-permute-start.7
  69.6 7.2 collective-permute-start.8
  75.4 5.6 collective-permute-start.9
  81.0 6.3 collective-permute-start.10
  84.3 5.4 collective-permute-start.11
  133.2 493.9 %all-reduce.13.cloned.1.call-start = ((), (), s32[]{:S(2)}) async-start(), calls=%async_computation | async-start | bytes 884736 | tf_op jit(solution)/shard_map/psum | solution.py:14
  381.0 12.2 %collective-permute-start.12 = (bf16[1,1,4,128]{3,2,1,0:T(4,128)(2,1)S(1)}, bf16[1,1,4,128]{3,2,1,0:T(4,128)(2,1)S(1)}, u32[]{:S(2)}, u32[]{:S(2)}) collective-permute-start(bf16[1,1,4,128]{3,2,1,0:T(4,128)(2,1)S(1)} %get-tuple-element.323), channel_id=1, source_target_pairs={{0,32},{32,64},{64,96},{96,128},{128,160},{160,192},{192,224},{224... | collective-permute-start | bytes 3080 | tf_op jit(solution)/shard_map/ppermute | solution.py:29
  385.5 7.7 collective-permute-start.13
  395.2 4.9 collective-permute-start.15
  407.7 8.3 collective-permute-start.16
  413.2 6.8 collective-permute-start.17
  416.0 438.8 %all-reduce.15.cloned.1.call-start = ((), (), s32[]{:S(2)}) async-start(), calls=%async_computation.1 | async-start | bytes 884736 | tf_op jit(solution)/shard_map/psum | solution.py:14
  420.0 5.8 collective-permute-start.19
  422.2 4.5 collective-permute-start.18
  625.2 5.6 collective-permute-start.21
  630.8 9.5 %collective-permute-start.23 = (bf16[32,6,1,128]{3,0,2,1:T(8,128)(2,1)S(1)}, bf16[32,6,1,128]{3,0,2,1:T(8,128)(2,1)S(1)}, u32[]{:S(2)}, u32[]{:S(2)}) collective-permute-start(bf16[32,6,1,128]{3,0,2,1:T(8,128)(2,1)S(1)} %get-tuple-element.156), channel_id=1, source_target_pairs={{1,0},{2,1},{3,2},{4,3},{5,4},{6,5},{7,6},{8,7},{9,8},{10,9},{11,1... | collective-permute-start | bytes 147464 | tf_op jit(solution)/shard_map/ppermute | solution.py:31
  (103 other events, 663.5 us)
Sparse Core Ops, SparseCore 0:
  133.4 228.6 all-reduce.16
  416.1 164.7 all-reduce.12
  627.3 227.4 all-reduce.14
